TPU v7x, 128 devices: a whole 4x4x4 slice. The times are simulated.
128 devices in a mesh: root: 4 (over z_lo, core), virt: 32 (over z_hi, y, x).
Axes of the slice: x: 4, y: 4, z: 4 (z_hi: 2, z_lo: 2; z = z_hi * 2 + z_lo), core: 2. Of those that a mesh axis runs over, the one named last changes fastest.
Arguments:
- r2: bfloat16 [512, 16384], P('virt', 'root'), parts along dimension 1, may hold values from -6 to 6
- tau: bfloat16 [512, 512, 3072], P('virt', None, 'root'), parts along dimension 2, may hold values from -6 to 6
- w_vvv: bfloat16 [512, 512, 512], P('virt'), may hold values from -0.01171875 to 0.01171875
- w_oooo: bfloat16 [768, 4096], P('virt'), may hold values from -0.09375 to 0.09375
- w_ovoo: bfloat16 [64, 768, 512], P(None, 'virt'), may hold values from -0.75 to 0.75
- fock_oo: bfloat16 [64, 64], replicated, may hold values from -0.75 to 0.75
- fock_vv: bfloat16 [512, 512], replicated, may hold values from -0.25 to 0.25
- r1: bfloat16 [256], P('root'), parts along dimension 0, may hold values from -6 to 6
Outputs:
- sigma: float32 [3072, 512], P(('root', 'virt')), parts along dimension 0
There are 4 independent parts, one for each index of `root`. A program takes and returns all parts, laid end to end along the dimension named above; an argument that names none is the same for every part. Nothing has to cross between parts.
All inputs are finite; a program needn't handle non-finite values.
Results may differ from a plain program's by a relative error of at most 0.0003.
Values may be sent and summed in bfloat16 or wider, within the bound.
A program may use at most 192 MiB of HBM per device.

v0:
```python
import jax
import jax.numpy as jnp
from jax import lax
from jax.sharding import PartitionSpec as P


def split_up(x, dim, devices):
    before, after = (x.shape[:dim], x.shape[dim + 1 :])
    return jnp.moveaxis(x.reshape(*before, devices, -1, *after), dim, 0)


def edges_of(length, count):
    unit = 8 if length >= 8 * count else 1
    return [length // unit * k // count * unit for k in range(1, count)]


def laid_out(blocks, dim):
    shape = list(blocks.shape[1:])
    shape[dim] *= blocks.shape[0]
    return jnp.moveaxis(blocks, 0, dim).reshape(shape)


def exchange_in_pieces(x, axis, pieces, split_dim, concat_dim):
    blocks = split_up(x, split_dim, lax.axis_size(axis))
    split_at = max(range(1, max(2, blocks.ndim - 1)), key=lambda d: blocks.shape[d])
    finished = []
    for section in jnp.split(blocks, edges_of(blocks.shape[split_at], pieces), axis=split_at):
        if section.size:
            finished.append(lax.all_to_all(section, axis, split_axis=0, concat_axis=0, tiled=True))
    return laid_out(jnp.concatenate(finished, axis=split_at), concat_dim)


def summed_on_arrival(x, axis, dim):
    blocks = split_up(x, dim, lax.axis_size(axis))
    arrived = lax.all_to_all(blocks, axis, split_axis=0, concat_axis=0, tiled=True)
    return arrived.sum(axis=0)


def local_terms(carried, segment, fock_vv, fock_oo, w_oooo, pair_first):
    segment_rows = segment.shape[0]
    occupied = fock_oo.shape[0]
    pair_rows = w_oooo.shape[0]
    window = lax.dynamic_slice_in_dim(segment, pair_first, pair_rows, 1)
    carried = jnp.einsum("ep,ae->pa", window, fock_vv, preferred_element_type=jnp.float32)
    cubic_view = segment.reshape(segment_rows, occupied, occupied)
    first_term = jnp.einsum("mi,amj->aij", fock_oo, cubic_view, preferred_element_type=jnp.float32)
    second_term = jnp.einsum("mj,aim->aij", fock_oo, cubic_view, preferred_element_type=jnp.float32)
    occ_part = (first_term + second_term).reshape(segment_rows, occupied * occupied)
    occ_window = lax.dynamic_slice_in_dim(occ_part, pair_first, pair_rows, 1)
    quartic = jnp.einsum("pk,ak->pa", w_oooo, segment, preferred_element_type=jnp.float32)
    update = quartic - occ_window.T
    return carried + update


def on_device(r2, tau, w_vvv, w_oooo, w_ovoo, fock_oo, fock_vv, r1):
    pair_rows = w_oooo.shape[0]
    pair_first = lax.axis_index("virt") * pair_rows
    initial = jnp.zeros((pair_rows, fock_vv.shape[0]), jnp.float32)
    folded = local_terms(
        initial,
        lax.all_gather(r2, "virt", axis=0, tiled=True),
        fock_vv,
        fock_oo,
        w_oooo,
        pair_first,
    )
    weights = exchange_in_pieces(w_vvv, "virt", 2, 1, 0)
    three_virtual = summed_on_arrival(
        jnp.einsum("bep,eba->pa", tau, weights, preferred_element_type=jnp.float32), "virt", 0
    )
    singles = jnp.dot(
        r1[None, :], w_ovoo.reshape(w_ovoo.shape[0], -1), preferred_element_type=jnp.float32
    ).reshape(pair_rows, -1)
    return three_virtual + folded - singles


def solution(mesh):
    in_specs = (
        P("virt", "root"),
        P("virt", None, "root"),
        P("virt", None, None),
        P("virt", None),
        P(None, "virt", None),
        P(),
        P(),
        P("root"),
    )
    out_specs = P(("root", "virt"), None)
    return jax.shard_map(
        on_device, mesh=mesh, in_specs=in_specs, out_specs=out_specs, check_vma=False
    )
```

profile of v0, /device:TPU:8, one launch (start us, length us, event | category | flops | bytes accessed | tf_op | source)
XLA Modules:
  0.0 248.4 jit_solution(11978240766337686828)
XLA Ops:
  6.5 0.0 copy-start
  6.5 5.4 %fusion.20 = (bf16[32,8,16,512]{3,2,0,1:T(8,128)(2,1)S(1)}, bf16[32,8,16,512]{3,2,0,1:T(8,128)(2,1)}) fusion(bf16[32,16,16,512]{3,2,0,1:T(8,128)(2,1)} %bitcast.45), kind=kLoop, calls=%fused_computation.20 | loop fusion | bytes 16777216 | tf_op jit(solution)/shard_map/split | solution.py:27
  11.9 2.4 copy.32
  14.4 10.9 %all-to-all-start = ((bf16[32,8,16,512]{3,2,1,0:T(8,128)(2,1)}), bf16[32,8,16,512]{3,2,1,0:T(8,128)(2,1)}, u32[]{:S(2)}, u32[]{:S(2)}) async-start(bf16[32,8,16,512]{3,2,1,0:T(8,128)(2,1)} %copy.32), calls=%async_computation | async-start | bytes 8388608 | tf_op jit(solution)/shard_map/all_to_all | solution.py:29
  25.3 4.8 %copy.33 = bf16[32,8,16,512]{3,2,1,0:T(8,128)(2,1)} copy(bf16[32,8,16,512]{3,2,0,1:T(8,128)(2,1)} %get-tuple-element.6) | data formatting | bytes 8388608 | tf_op jit(solution)/shard_map/split | solution.py:27
  30.1 47.0 %all-to-all-done = bf16[32,8,16,512]{3,2,1,0:T(8,128)(2,1)} async-done(((bf16[32,8,16,512]{3,2,1,0:T(8,128)(2,1)}), bf16[32,8,16,512]{3,2,1,0:T(8,128)(2,1)}, u32[]{:S(2)}, u32[]{:S(2)}) %all-to-all-start) | async-done | bytes 4194336 | tf_op jit(solution)/shard_map/all_to_all | solution.py:29
  77.1 9.5 %all-to-all-start.1 = ((bf16[32,8,16,512]{3,2,1,0:T(8,128)(2,1)}), bf16[32,8,16,512]{3,2,1,0:T(8,128)(2,1)}, u32[]{:S(2)}, u32[]{:S(2)}) async-start(bf16[32,8,16,512]{3,2,1,0:T(8,128)(2,1)} %copy.33), calls=%async_computation.1 | async-start | bytes 8388608 | tf_op jit(solution)/shard_map/all_to_all | solution.py:29
  86.6 0.0 all-gather.2.cloned.1.call-start
  86.6 0.7 all-gather.2.cloned.1.call-update
  87.3 50.1 %all-to-all-done.1 = bf16[32,8,16,512]{3,2,1,0:T(8,128)(2,1)} async-done(((bf16[32,8,16,512]{3,2,1,0:T(8,128)(2,1)}), bf16[32,8,16,512]{3,2,1,0:T(8,128)(2,1)}, u32[]{:S(2)}, u32[]{:S(2)}) %all-to-all-start.1) | async-done | bytes 4194336 | tf_op jit(solution)/shard_map/all_to_all | solution.py:29
  137.4 7.4 %pad_maximum_fusion = bf16[32,16,16,512]{3,2,1,0:T(8,128)(2,1)} fusion(bf16[32,8,16,512]{3,2,1,0:T(8,128)(2,1)} %all-to-all-done.1, bf16[32,8,16,512]{3,2,1,0:T(8,128)(2,1)} %all-to-all-done), kind=kLoop, calls=%fused_computation.2 | loop fusion | flops 4194304 | bytes 16777216 | tf_op jit(solution)/shard_map/concatenate | solution.py:30
  144.9 16.5 %fusion.9 = f32[768,512]{0,1:T(8,128)S(1)} fusion(bf16[512,16,512]{2,1,0:T(8,128)(2,1)} %bitcast.46, bf16[16,512,768]{2,1,0:T(8,128)(2,1)} %param.9), kind=kOutput, calls=%fused_computation.9 | convolution fusion | flops 6442450944 | bytes 22544384 | tf_op jit(solution)/shard_map/bep,eba->pa/dot_general | solution.py:69
  161.3 0.0 copy-start.5
  161.4 1.6 copy.35
  163.0 10.0 %all-to-all-start.2 = ((f32[32,24,512]{2,1,0:T(8,128)}), f32[32,24,512]{2,1,0:T(8,128)S(1)}, u32[]{:S(2)}, u32[]{:S(2)}) async-start(f32[32,24,512]{2,1,0:T(8,128)} %bitcast.47), calls=%async_computation.2 | async-start | bytes 3145728 | tf_op jit(solution)/shard_map/all_to_all | solution.py:35
  173.0 0.0 copy-done.5
  173.0 2.0 fusion.6
  175.0 22.1 %all-to-all-done.2 = f32[32,24,512]{2,1,0:T(8,128)S(1)} async-done(((f32[32,24,512]{2,1,0:T(8,128)}), f32[32,24,512]{2,1,0:T(8,128)S(1)}, u32[]{:S(2)}, u32[]{:S(2)}) %all-to-all-start.2) | async-done | bytes 1572896 | tf_op jit(solution)/shard_map/all_to_all | solution.py:35
  197.1 0.1 reduce_sum.9
  197.2 0.0 copy-start.4
  197.2 18.9 %all-gather.2.cloned.1.call-done = bf16[512,4096]{1,0:T(8,128)(2,1)} async-done(((bf16[16,4096]{1,0:T(8,128)(2,1)}), bf16[512,4096]{1,0:T(8,128)(2,1)}) %all-gather.2.cloned.1.call-update) | async-done | bytes 4194320 | tf_op jit(solution)/shard_map/all_gather | solution.py:61
  216.1 6.5 %copy.36 = bf16[512,4096]{0,1:T(8,128)(2,1)} copy(bf16[512,4096]{1,0:T(8,128)(2,1)} %all-gather.2.cloned.1.call-done) | data formatting | bytes 8388608 | tf_op jit(solution)/shard_map/all_gather | solution.py:61
  222.6 0.0 copy-done.4
  222.6 3.8 %fusion.15 = f32[512,64,64]{0,2,1:T(8,128)S(1)} fusion(bf16[512,64,64]{0,2,1:T(8,128)(2,1)} %bitcast.42, bf16[64,64]{1,0:T(8,128)(2,1)S(1)} %copy-done.4), kind=kOutput, calls=%fused_computation.15 | convolution fusion | flops 268435456 | bytes 12591104 | tf_op jit(solution)/shard_map/mj,aim->aij/dot_general | solution.py:47
  226.4 0.0 copy-done.1
  226.4 8.0 %bitcast_add_fusion = f32[512,64,64]{0,1,2:T(8,128)S(1)} fusion(f32[512,64,64]{0,2,1:T(8,128)S(1)} %fusion.15, bf16[512,64,64]{0,2,1:T(8,128)(2,1)S(1)} %bitcast.43, bf16[64,64]{1,0:T(8,128)(2,1)S(1)} %copy-done.4), kind=kOutput, calls=%fused_computation.3 | convolution fusion | flops 270532608 | bytes 20979712 | tf_op jit(solution)/shard_map/mi,amj->aij/dot_general | solution.py:46
  234.4 0.0 copy-start.2
  234.4 0.0 copy-start.3
  234.5 4.9 %copy.41 = f32[512,64,64]{0,2,1:T(8,128)S(1)} copy(f32[512,64,64]{0,1,2:T(8,128)S(1)} %bitcast_add_fusion) | data formatting | bytes 16777216 | tf_op jit(solution)/shard_map/add | solution.py:48
  239.3 1.2 convolution_subtract_fusion
  240.5 0.0 copy-done
  240.5 1.0 fusion.13
  (3 shorter events, 0.0 us)
Async XLA Ops:
  6.5 234.0 %copy-start = (bf16[512,512]{1,0:T(8,128)(2,1)S(1)}, bf16[512,512]{1,0:T(8,128)(2,1)}, u32[]{:S(2)}) copy-start(bf16[512,512]{1,0:T(8,128)(2,1)} %param.14) | copy-start | bytes 1572868
  14.4 62.7 %all-to-all-start = ((bf16[32,8,16,512]{3,2,1,0:T(8,128)(2,1)}), bf16[32,8,16,512]{3,2,1,0:T(8,128)(2,1)}, u32[]{:S(2)}, u32[]{:S(2)}) async-start(bf16[32,8,16,512]{3,2,1,0:T(8,128)(2,1)} %copy.32), calls=%async_computation | async-start | bytes 8388608 | tf_op jit(solution)/shard_map/all_to_all | solution.py:29
  77.1 60.3 %all-to-all-start.1 = ((bf16[32,8,16,512]{3,2,1,0:T(8,128)(2,1)}), bf16[32,8,16,512]{3,2,1,0:T(8,128)(2,1)}, u32[]{:S(2)}, u32[]{:S(2)}) async-start(bf16[32,8,16,512]{3,2,1,0:T(8,128)(2,1)} %copy.33), calls=%async_computation.1 | async-start | bytes 8388608 | tf_op jit(solution)/shard_map/all_to_all | solution.py:29
  86.6 129.5 %all-gather.2.cloned.1.call-start = ((), (), s32[]{:S(2)}) async-start(), calls=%async_computation.3 | async-start | bytes 4325376 | tf_op jit(solution)/shard_map/all_gather | solution.py:61
  161.3 11.7 %copy-start.5 = (bf16[64]{0:T(256)(128)(2,1)S(1)}, bf16[64]{0:T(256)(128)(2,1)}, u32[]{:S(2)}) copy-start(bf16[64]{0:T(256)(128)(2,1)} %param.15) | copy-start | bytes 388
  163.0 34.1 %all-to-all-start.2 = ((f32[32,24,512]{2,1,0:T(8,128)}), f32[32,24,512]{2,1,0:T(8,128)S(1)}, u32[]{:S(2)}, u32[]{:S(2)}) async-start(f32[32,24,512]{2,1,0:T(8,128)} %bitcast.47), calls=%async_computation.2 | async-start | bytes 3145728 | tf_op jit(solution)/shard_map/all_to_all | solution.py:35
  197.2 25.3 %copy-start.4 = (bf16[64,64]{1,0:T(8,128)(2,1)S(1)}, bf16[64,64]{1,0:T(8,128)(2,1)}, u32[]{:S(2)}) copy-start(bf16[64,64]{1,0:T(8,128)(2,1)} %param.13) | copy-start | bytes 24580
  222.6 3.8 %copy-start.1 = (bf16[512,4096]{0,1:T(8,128)(2,1)S(1)}, bf16[512,4096]{0,1:T(8,128)(2,1)}, u32[]{:S(2)}) copy-start(bf16[512,4096]{0,1:T(8,128)(2,1)} %copy.36) | copy-start | bytes 12582916
  234.4 4.9 %copy-start.2 = (bf16[512,4096]{1,0:T(8,128)(2,1)S(1)}, bf16[512,4096]{1,0:T(8,128)(2,1)}, u32[]{:S(2)}) copy-start(bf16[512,4096]{1,0:T(8,128)(2,1)} %all-gather.2.cloned.1.call-done) | copy-start | bytes 12582916
  234.4 4.9 %copy-start.3 = (bf16[24,4096]{1,0:T(8,128)(2,1)S(1)}, bf16[24,4096]{1,0:T(8,128)(2,1)}, u32[]{:S(2)}) copy-start(bf16[24,4096]{1,0:T(8,128)(2,1)} %param.11) | copy-start | bytes 589828
Sparse Core Ops, SparseCore 0:
  90.4 125.6 all-gather.1
where the time goes:
time: 250 us; the launch traced here: 248 us
  waiting for transfers between devices  139 us (56%)
  matrix products  32.5 us (13%)
  starting transfers between devices  30.4 us (12%)
  local copies, waits for them, and re-layouts  25.6 us (10%)
  between operations  13.5 us (5%)
  other arithmetic  7.52 us (3%)
    all_to_all x2, waiting for transfers between devices, exchange_in_pieces(): lax.all_to_all(section, axis, split_axis=0, concat_axis=0, tiled=True)  97.2 us
    all_to_all x1, waiting for transfers between devices, summed_on_arrival(): lax.all_to_all(blocks, axis, split_axis=0, concat_axis=0, tiled=True)  22.1 us
    all_to_all x2, starting transfers between devices, exchange_in_pieces(): lax.all_to_all(section, axis, split_axis=0, concat_axis=0, tiled=True)  20.4 us
    all_gather x1, waiting for transfers between devices, on_device(): lax.all_gather(r2, 'virt', axis=0, tiled=True)  18.9 us
    dot_general x1, matrix products, on_device(): jnp.einsum('bep,eba->pa', tau, weights, preferred_element_type=jnp.float32)  16.5 us
    split x3, local copies, waits for them, and re-layouts, exchange_in_pieces(): jnp.split(blocks, edges_of(blocks.shape[split_at], pieces), axis=split_at)  12.6 us
    all_to_all x1, starting transfers between devices, summed_on_arrival(): lax.all_to_all(blocks, axis, split_axis=0, concat_axis=0, tiled=True)  10 us
    dot_general x1, matrix products, local_terms(): jnp.einsum('mi,amj->aij', fock_oo, cubic_view, preferred_element_type=jnp...  8.02 us
  transfers between devices with their start and end apart: 4, of which 4 were waited for; matrix products, arithmetic and copies ran while one was open for 13% of the time, Pallas kernels for 0%

commit v1 on v0

v1 whole, which is shorter than its diff:
```python
import functools
import math

import jax
import jax.numpy as jnp
from jax import lax
from jax.experimental import pallas as pl
from jax.experimental.pallas import tpu as pltpu
from jax.sharding import PartitionSpec as P

MESH = pl.DeviceIdType.MESH
F32, BF16 = jnp.float32, jnp.bfloat16
EB = 16
HALF = 8
LONG = 5
SHARE = 3
SLOTS = 4
LAG = 2


def dot(a, b, ca, cb):
    return lax.dot_general(a, b, (((ca,), (cb,)), ((), ())), preferred_element_type=F32)


def iotas(rows, cols):
    return (lax.broadcasted_iota(jnp.int32, (rows, cols), 0), lax.broadcasted_iota(jnp.int32, (rows, cols), 1))


def onehot(mask):
    return jnp.where(mask, 1.0, 0.0).astype(BF16)


def kernel(
    ny, nx,
    r2, tau, w, wo, wov, foo, fvv, r1,
    out,
    wbuf, tbuf, acc, rbuf, wovb, r2s, wos, foob, fvvb, winb, r1b, sing, perm,
    tau_sem, loc_sem, long_send, long_recv, z_send, z_recv, sib_send, sib_recv, small_send, small_recv, rs_send, rs_recv,
):
    nv = 2 * ny * nx
    nocc = foo.shape[0]
    pairs = tau.shape[2]
    rows = pairs // nv
    cw = wo.shape[1] // nv
    virt = fvv.shape[0]
    ob = int(math.log2(nocc))
    root, me = lax.axis_index("root"), lax.axis_index("virt")
    zl, c = root // 2, root % 2
    zh, y, x = me // (ny * nx), (me // nx) % ny, me % nx
    sibling = (zl * 2 + 1 - c, me)
    partner = ((1 - zl) * 2 + c, me)

    def peer(j, sign):
        k = (j * 13) % nv
        oz, oy, ox = k // (ny * nx), (k // nx) % ny, k % nx
        v = ((zh + oz) % 2) * (ny * nx) + ((y + sign * oy + ny) % ny) * nx + (x + sign * ox + nx) % nx
        return v, (zl + oz) % 2

    def tau_copy(j):
        v, _ = peer(j, -1)
        return pltpu.make_async_copy(
            tau.at[:, pl.ds(pl.multiple_of(v * EB, EB), EB), :], tbuf.at[j % SLOTS], tau_sem.at[j % SLOTS]
        )

    mine = pl.ds(pl.multiple_of(me * EB, EB), EB)
    my_cols = pl.ds(pl.multiple_of(me * cw, cw), cw)
    local = [
        pltpu.make_async_copy(w.at[:, mine, :], wbuf.at[0], loc_sem.at[0]),
        pltpu.make_async_copy(wov, wovb, loc_sem.at[1]),
        pltpu.make_async_copy(foo, foob, loc_sem.at[2]),
        pltpu.make_async_copy(fvv, fvvb, loc_sem.at[3]),
        pltpu.make_async_copy(r2.at[:, pl.ds(0, pairs)], winb, loc_sem.at[4]),
        pltpu.make_async_copy(r2.at[:, my_cols], r2s.at[mine, :], loc_sem.at[5]),
        pltpu.make_async_copy(wo.at[:, my_cols], wos.at[me], loc_sem.at[6]),
        pltpu.make_async_copy(r1, r1b, loc_sem.at[7]),
    ]

    barrier = pltpu.get_barrier_semaphore()

    def greet(j, _):
        v, zd = peer(j, 1)
        pl.semaphore_signal(barrier, inc=1, device_id=(root, v), device_id_type=MESH)

        @pl.when(zd != zl)
        def _():
            pl.semaphore_signal(barrier, inc=1, device_id=(zd * 2 + c, v), device_id_type=MESH)

        return 0

    lax.fori_loop(1, nv, greet, 0)
    for other in (sibling, partner):
        pl.semaphore_signal(barrier, inc=1, device_id=other, device_id_type=MESH)
    for copy in local:
        copy.start()
    for j in range(LAG):
        tau_copy(j).start()
    pl.semaphore_wait(barrier, nv - 1 + nv // 2 + 2)

    def small_copies(v):
        cols = pl.ds(pl.multiple_of(v * cw, cw), cw)
        return (
            pltpu.make_async_remote_copy(
                src_ref=r2.at[:, cols], dst_ref=r2s.at[mine, :], send_sem=small_send.at[0], recv_sem=small_recv.at[0],
                device_id=(root, v), device_id_type=MESH,
            ),
            pltpu.make_async_remote_copy(
                src_ref=wo.at[:, cols], dst_ref=wos.at[me], send_sem=small_send.at[1], recv_sem=small_recv.at[1],
                device_id=(root, v), device_id_type=MESH,
            ),
        )

    def send(j, _):
        v, zd = peer(j, 1)
        first = HALF * c + SHARE * zd
        pltpu.make_async_remote_copy(
            src_ref=w.at[pl.ds(first, LONG), pl.ds(pl.multiple_of(v * EB, EB), EB), :],
            dst_ref=wbuf.at[j, pl.ds(first, LONG)],
            send_sem=long_send.at[0],
            recv_sem=long_recv.at[j],
            device_id=(zd * 2 + c, v),
            device_id_type=MESH,
        ).start()
        for copy in small_copies(v):
            copy.start()
        return 0

    lax.fori_loop(1, nv, send, 0)

    i, j = iotas(EB * EB, EB * EB)
    perm[...] = onehot(((i >> 4) == (j & 15)) & ((i & 15) == (j >> 4)))

    local[3].wait()
    local[4].wait()
    i, j = iotas(EB, virt)
    chosen = dot(onehot(j == i + me * EB), fvvb[...], 1, 1).astype(BF16)
    acc[...] = dot(winb[...], chosen, 0, 0)

    def z_copy(j):
        part = wbuf.at[j, pl.ds(HALF * c + LONG * zl, SHARE)]
        return pltpu.make_async_remote_copy(
            src_ref=part, dst_ref=part, send_sem=z_send.at[0], recv_sem=z_recv.at[j], device_id=partner, device_id_type=MESH
        )

    def sib_copy(j):
        part = wbuf.at[j, pl.ds(HALF * c, HALF)]
        return pltpu.make_async_remote_copy(
            src_ref=part, dst_ref=part, send_sem=sib_send.at[0], recv_sem=sib_recv.at[j], device_id=sibling, device_id_type=MESH
        )

    def received(ref, sem):
        pltpu.make_async_copy(ref, ref, sem).wait()

    def compute(j):
        tau_copy(j).wait()
        block = tbuf[j % SLOTS].reshape(EB * EB, pairs)
        turned = dot(perm[...], block, 1, 0).astype(BF16)
        weights = wbuf[j].reshape(EB * EB, virt)
        step = pairs // 3
        for part in range(3):
            at = slice(part * step, (part + 1) * step)
            acc[at, :] += dot(turned[:, at], weights, 0, 0)

    def advance(j, _):
        @pl.when(j + LAG < nv)
        def _():
            tau_copy(j + LAG).start()

        @pl.when(j + 2 < nv)
        def _():
            received(wbuf.at[j + 2, pl.ds(HALF * c + SHARE * zl, LONG)], long_recv.at[j + 2])
            z_copy(j + 2).start()

        @pl.when((j + 1 < nv) & (j + 1 > 0))
        def _():
            received(wbuf.at[j + 1, pl.ds(HALF * c + LONG * (1 - zl), SHARE)], z_recv.at[j + 1])
            sib_copy(j + 1).start()

        @pl.when(j > 0)
        def _():
            received(wbuf.at[j, pl.ds(HALF * (1 - c), HALF)], sib_recv.at[j])

        compute(j)
        return 0

    received(wbuf.at[1, pl.ds(HALF * c + SHARE * zl, LONG)], long_recv.at[1])
    z_copy(1).start()
    local[0].wait()
    middle = nv // 2
    lax.fori_loop(0, middle, advance, 0)

    local[1].wait()
    local[7].wait()
    i, j = iotas(nocc, nocc)
    spread = jnp.where(i == j, jnp.broadcast_to(r1b[...].astype(F32), (nocc, nocc)), 0.0).astype(BF16)
    winb32 = dot(spread, jnp.ones((nocc, 128), BF16), 1, 0)
    sing[...] = jnp.zeros_like(sing)
    for k in range(nocc):
        factor = jnp.broadcast_to(winb32[k : k + 1, 0:1], (rows, virt))
        sing[...] += factor * wovb[k].astype(F32)

    local[2].wait()
    local[5].wait()
    local[6].wait()
    others = (nv - 1) * EB
    received(r2s.at[pl.ds(0, others), :], small_recv.at[0])
    received(wos.at[pl.ds(0, nv - 1)], small_recv.at[1])
    held = r2s[...]
    fock = foob[...]
    m_first = me * (cw // nocc)
    i, j = iotas(nocc, cw)
    by_i = dot(fock, onehot(i == (j >> ob) + m_first), 0, 0).astype(BF16)
    by_j = dot(fock, onehot(i == (j & (nocc - 1))), 0, 0).astype(BF16)
    p, q = iotas(pairs, nocc)
    take_i = dot(onehot((p >> ob) == q), by_i, 1, 0)
    take_j = dot(onehot((p & (nocc - 1)) == q), by_j, 1, 0)
    p, q = iotas(pairs, cw)
    first = jnp.where((p & (nocc - 1)) == (q & (nocc - 1)), take_i, 0.0).astype(BF16)
    second = jnp.where((p >> ob) == (q >> ob) + m_first, take_j, 0.0).astype(BF16)
    quartic = wos[...].astype(F32).reshape(pairs, cw).astype(BF16)
    acc[...] += dot(quartic, held, 1, 1) - dot(first, held, 1, 1) - dot(second, held, 1, 1)

    lax.fori_loop(middle, nv, advance, 0)

    def share(j, _):
        v, _zd = peer(j, 1)
        pltpu.make_async_remote_copy(
            src_ref=acc.at[pl.ds(pl.multiple_of(v * rows, 8), rows), :],
            dst_ref=rbuf.at[j],
            send_sem=rs_send.at[0],
            recv_sem=rs_recv.at[0],
            device_id=(root, v),
            device_id_type=MESH,
        ).start()
        return 0

    lax.fori_loop(1, nv, share, 0)
    sing[...] = acc[pl.ds(pl.multiple_of(me * rows, 8), rows), :] - sing[...]
    received(wbuf.at[pl.ds(0, nv - 1), pl.ds(0, LONG)], long_send.at[0])
    received(wbuf.at[pl.ds(0, nv - 1), pl.ds(0, SHARE)], z_send.at[0])
    received(wbuf.at[pl.ds(0, nv - 1), pl.ds(0, HALF)], sib_send.at[0])
    received(r2s.at[pl.ds(0, others), :], small_send.at[0])
    received(wos.at[pl.ds(0, nv - 1)], small_send.at[1])
    received(rbuf.at[pl.ds(1, nv - 1)], rs_recv.at[0])
    out[...] = sing[...] + jnp.sum(rbuf[pl.ds(1, nv - 1)], axis=0)
    received(rbuf.at[pl.ds(1, nv - 1)], rs_send.at[0])


def on_device(r2, tau, w, wo, wov, foo, fvv, r1):
    nv = w.shape[1] // w.shape[0]
    side = int(math.isqrt(nv // 2))
    rows, virt, pairs, nocc = wo.shape[0], w.shape[2], tau.shape[2], foo.shape[0]
    cw = wo.shape[1] // nv
    dma = pltpu.SemaphoreType.DMA
    flops = 2 * nv * EB * EB * pairs * (virt + EB * EB)
    return pl.pallas_call(
        functools.partial(kernel, side, side),
        out_shape=jax.ShapeDtypeStruct((rows, virt), F32),
        in_specs=[pl.BlockSpec(memory_space=pl.ANY)] * 8,
        out_specs=pl.BlockSpec(memory_space=pltpu.VMEM),
        scratch_shapes=[
            pltpu.VMEM((nv, EB, EB, virt), BF16),
            pltpu.VMEM((SLOTS, EB, EB, pairs), BF16),
            pltpu.VMEM((pairs, virt), F32),
            pltpu.VMEM((nv, rows, virt), F32),
            pltpu.VMEM((nocc, rows, virt), BF16),
            pltpu.VMEM((virt, cw), BF16),
            pltpu.VMEM((nv, rows, cw), BF16),
            pltpu.VMEM((nocc, nocc), BF16),
            pltpu.VMEM((virt, virt), BF16),
            pltpu.VMEM((EB, pairs), BF16),
            pltpu.VMEM((1, nocc), BF16),
            pltpu.VMEM((rows, virt), F32),
            pltpu.VMEM((EB * EB, EB * EB), BF16),
            dma((SLOTS,)), dma((8,)),
            dma((1,)), dma((nv,)), dma((1,)), dma((nv,)), dma((1,)), dma((nv,)),
            dma((2,)), dma((2,)), dma((1,)), dma((1,)),
        ],
        compiler_params=pltpu.CompilerParams(collective_id=0, has_side_effects=True, vmem_limit_bytes=56 * 2**20),
        cost_estimate=pl.CostEstimate(flops=flops, bytes_accessed=26_000_000, transcendentals=0),
        name="ladder",
    )(r2, tau, w, wo, wov, foo, fvv, r1.reshape(1, -1))


def solution(mesh):
    in_specs = (
        P("virt", "root"),
        P("virt", None, "root"),
        P("virt", None, None),
        P("virt", None),
        P(None, "virt", None),
        P(),
        P(),
        P("root"),
    )
    return jax.shard_map(
        on_device, mesh=mesh, in_specs=in_specs, out_specs=P(("root", "virt"), None), check_vma=False
    )
```

time: 250 us -> 110 us (0.44)
  the two profiles are of different devices: /device:TPU:8 before, /device:TPU:1 now
where the time goes in v1:
time: 110 us
  Pallas kernels  109 us (99%)
  local copies, waits for them, and re-layouts  1.42 us (1%)
    pallas_call x1, Pallas kernels, on_device(): pl.pallas_call(functools.partial(kernel, side, side), out_shape=jax.Shape...  109 us

profile of v1, /device:TPU:1, one launch (start us, length us, event | category | flops | bytes accessed | tf_op | source)
XLA Modules:
  0.0 110.3 jit_solution(10381580029709039908)
XLA Ops:
  0.0 108.9 %ladder.1 = f32[24,512]{1,0:T(8,128)} custom-call(bf16[16,4096]{1,0:T(8,128)(2,1)} %r2.1, bf16[16,512,768]{2,1,0:T(8,128)(2,1)} %tau.1, bf16[16,512,512]{2,1,0:T(8,128)(2,1)} %w.1, bf16[24,4096]{1,0:T(8,128)(2,1)} %wo.1, bf16[64,24,512]{2,1,0:T(8,128)(2,1)} %wov.1, bf16[64,64]{1,0:T(8,128)(2,1)} %foo.1, bf16[512,512]{1,0:T(8,128)(2,1)} %fvv.1, ...), custom_call_target="tpu_custom_call" | custom-call | flops 9663676416 | bytes 26000000 | tf_op jit(solution)/shard_map/ladder/pallas_call | solution.py:255
  108.9 1.4 %copy.10 = f32[24,512]{1,0:T(8,128)} copy(f32[24,512]{1,0:T(8,128)} %ladder.1) | data formatting | bytes 98304

commit v2 on v1

--- a/solution.py
+++ b/solution.py
@@ -14,8 +14,10 @@
 HALF = 8
 LONG = 5
 SHARE = 3
-SLOTS = 4
-LAG = 2
+SLOTS = 8
+Z_LAG = 3
+S_LAG = 3
+LAG = Z_LAG + S_LAG
 
 
 def dot(a, b, ca, cb):
@@ -34,7 +36,7 @@
     ny, nx,
     r2, tau, w, wo, wov, foo, fvv, r1,
     out,
-    wbuf, tbuf, acc, rbuf, wovb, r2s, wos, foob, fvvb, winb, r1b, sing, perm,
+    wbuf, tbuf, acc, first_x, first_y, total_x, total_y, last_x, last_y, wovb, r2s, wos, foob, fvvb, winb, r1b, sing, perm,
     tau_sem, loc_sem, long_send, long_recv, z_send, z_recv, sib_send, sib_recv, small_send, small_recv, rs_send, rs_recv,
 ):
     nv = 2 * ny * nx
@@ -92,8 +94,6 @@
         pl.semaphore_signal(barrier, inc=1, device_id=other, device_id_type=MESH)
     for copy in local:
         copy.start()
-    for j in range(LAG):
-        tau_copy(j).start()
     pl.semaphore_wait(barrier, nv - 1 + nv // 2 + 2)
 
     def small_copies(v):
@@ -133,7 +133,7 @@
     local[4].wait()
     i, j = iotas(EB, virt)
     chosen = dot(onehot(j == i + me * EB), fvvb[...], 1, 1).astype(BF16)
-    acc[...] = dot(winb[...], chosen, 0, 0)
+    acc[...] = dot(winb[...], chosen, 0, 0).reshape(acc.shape)
 
     def z_copy(j):
         part = wbuf.at[j, pl.ds(HALF * c + LONG * zl, SHARE)]
@@ -155,35 +155,38 @@
         block = tbuf[j % SLOTS].reshape(EB * EB, pairs)
         turned = dot(perm[...], block, 1, 0).astype(BF16)
         weights = wbuf[j].reshape(EB * EB, virt)
-        step = pairs // 3
-        for part in range(3):
+        step = pairs // 2
+        for part in range(2):
             at = slice(part * step, (part + 1) * step)
-            acc[at, :] += dot(turned[:, at], weights, 0, 0)
+            acc[part] += dot(turned[:, at], weights, 0, 0).reshape(acc.shape[1:])
 
     def advance(j, _):
-        @pl.when(j + LAG < nv)
-        def _():
-            tau_copy(j + LAG).start()
-
-        @pl.when(j + 2 < nv)
-        def _():
-            received(wbuf.at[j + 2, pl.ds(HALF * c + SHARE * zl, LONG)], long_recv.at[j + 2])
-            z_copy(j + 2).start()
-
-        @pl.when((j + 1 < nv) & (j + 1 > 0))
-        def _():
-            received(wbuf.at[j + 1, pl.ds(HALF * c + LONG * (1 - zl), SHARE)], z_recv.at[j + 1])
-            sib_copy(j + 1).start()
-
-        @pl.when(j > 0)
-        def _():
-            received(wbuf.at[j, pl.ds(HALF * (1 - c), HALF)], sib_recv.at[j])
-
-        compute(j)
-        return 0
-
-    received(wbuf.at[1, pl.ds(HALF * c + SHARE * zl, LONG)], long_recv.at[1])
-    z_copy(1).start()
+        k, t = j - Z_LAG, j - LAG
+
+        @pl.when(j < nv)
+        def _():
+            tau_copy(j).start()
+
+        @pl.when((j >= 1) & (j < nv))
+        def _():
+            received(wbuf.at[j, pl.ds(HALF * c + SHARE * zl, LONG)], long_recv.at[j])
+            z_copy(j).start()
+
+        @pl.when((k >= 1) & (k < nv))
+        def _():
+            received(wbuf.at[k, pl.ds(HALF * c + LONG * (1 - zl), SHARE)], z_recv.at[k])
+            sib_copy(k).start()
+
+        @pl.when(t > 0)
+        def _():
+            received(wbuf.at[t, pl.ds(HALF * (1 - c), HALF)], sib_recv.at[t])
+
+        @pl.when(t >= 0)
+        def _():
+            compute(lax.max(t, 0))
+
+        return 0
+
     local[0].wait()
     middle = nv // 2
     lax.fori_loop(0, middle, advance, 0)
@@ -217,39 +220,81 @@
     first = jnp.where((p & (nocc - 1)) == (q & (nocc - 1)), take_i, 0.0).astype(BF16)
     second = jnp.where((p >> ob) == (q >> ob) + m_first, take_j, 0.0).astype(BF16)
     quartic = wos[...].astype(F32).reshape(pairs, cw).astype(BF16)
-    acc[...] += dot(quartic, held, 1, 1) - dot(first, held, 1, 1) - dot(second, held, 1, 1)
-
-    lax.fori_loop(middle, nv, advance, 0)
-
-    def share(j, _):
-        v, _zd = peer(j, 1)
+    other_terms = dot(quartic, held, 1, 1) - dot(first, held, 1, 1) - dot(second, held, 1, 1)
+    acc[...] += other_terms.reshape(acc.shape)
+
+    lax.fori_loop(middle, nv + LAG, advance, 0)
+
+    half = virt // 2
+    left, right = pl.ds(0, half), pl.ds(half, half)
+
+    def flat(z_at, y_at, x_at):
+        return z_at * (ny * nx) + y_at * nx + x_at
+
+    def along_x(ox):
+        at = (x + ox) % nx
+        return pltpu.make_async_remote_copy(
+            src_ref=acc.at[:, :, at, :, left], dst_ref=first_x.at[ox - 1], send_sem=rs_send.at[0], recv_sem=rs_recv.at[0],
+            device_id=(root, flat(zh, y, at)), device_id_type=MESH,
+        )
+
+    def along_y(oy):
+        at = (y + oy) % ny
+        return pltpu.make_async_remote_copy(
+            src_ref=acc.at[:, at, :, :, right], dst_ref=first_y.at[oy - 1], send_sem=rs_send.at[1], recv_sem=rs_recv.at[1],
+            device_id=(root, flat(zh, at, x)), device_id_type=MESH,
+        )
+
+    for offset in range(1, max(nx, ny)):
+        if offset < nx:
+            along_x(offset).start()
+        if offset < ny:
+            along_y(offset).start()
+
+    received(first_x, rs_recv.at[0])
+    total_x[...] = acc[:, :, x, :, :half] + jnp.sum(first_x[...], axis=0)
+
+    def to_owner_x(q, _):
+        z_at, y_at = (zh + q // ny) % 2, (y + q % ny) % ny
         pltpu.make_async_remote_copy(
-            src_ref=acc.at[pl.ds(pl.multiple_of(v * rows, 8), rows), :],
-            dst_ref=rbuf.at[j],
-            send_sem=rs_send.at[0],
-            recv_sem=rs_recv.at[0],
-            device_id=(root, v),
-            device_id_type=MESH,
+            src_ref=total_x.at[z_at, y_at], dst_ref=last_x.at[q - 1], send_sem=rs_send.at[2], recv_sem=rs_recv.at[2],
+            device_id=(root, flat(z_at, y_at, x)), device_id_type=MESH,
         ).start()
         return 0
 
-    lax.fori_loop(1, nv, share, 0)
-    sing[...] = acc[pl.ds(pl.multiple_of(me * rows, 8), rows), :] - sing[...]
+    lax.fori_loop(1, 2 * ny, to_owner_x, 0)
+    received(first_y, rs_recv.at[1])
+    total_y[...] = acc[:, y, :, :, half:] + jnp.sum(first_y[...], axis=0)
+
+    def to_owner_y(q, _):
+        z_at, x_at = (zh + q // nx) % 2, (x + q % nx) % nx
+        pltpu.make_async_remote_copy(
+            src_ref=total_y.at[z_at, x_at], dst_ref=last_y.at[q - 1], send_sem=rs_send.at[3], recv_sem=rs_recv.at[3],
+            device_id=(root, flat(z_at, y, x_at)), device_id_type=MESH,
+        ).start()
+        return 0
+
+    lax.fori_loop(1, 2 * nx, to_owner_y, 0)
     received(wbuf.at[pl.ds(0, nv - 1), pl.ds(0, LONG)], long_send.at[0])
     received(wbuf.at[pl.ds(0, nv - 1), pl.ds(0, SHARE)], z_send.at[0])
     received(wbuf.at[pl.ds(0, nv - 1), pl.ds(0, HALF)], sib_send.at[0])
     received(r2s.at[pl.ds(0, others), :], small_send.at[0])
     received(wos.at[pl.ds(0, nv - 1)], small_send.at[1])
-    received(rbuf.at[pl.ds(1, nv - 1)], rs_recv.at[0])
-    out[...] = sing[...] + jnp.sum(rbuf[pl.ds(1, nv - 1)], axis=0)
-    received(rbuf.at[pl.ds(1, nv - 1)], rs_send.at[0])
+    received(first_x, rs_send.at[0])
+    received(first_y, rs_send.at[1])
+    received(last_x, rs_recv.at[2])
+    out[:, :half] = total_x[zh, y] - sing[:, :half] + jnp.sum(last_x[...], axis=0)
+    received(last_y, rs_recv.at[3])
+    out[:, half:] = total_y[zh, x] - sing[:, half:] + jnp.sum(last_y[...], axis=0)
+    received(last_x, rs_send.at[2])
+    received(last_y, rs_send.at[3])
 
 
 def on_device(r2, tau, w, wo, wov, foo, fvv, r1):
     nv = w.shape[1] // w.shape[0]
     side = int(math.isqrt(nv // 2))
     rows, virt, pairs, nocc = wo.shape[0], w.shape[2], tau.shape[2], foo.shape[0]
-    cw = wo.shape[1] // nv
+    cw, half = wo.shape[1] // nv, virt // 2
     dma = pltpu.SemaphoreType.DMA
     flops = 2 * nv * EB * EB * pairs * (virt + EB * EB)
     return pl.pallas_call(
@@ -260,8 +305,13 @@
         scratch_shapes=[
             pltpu.VMEM((nv, EB, EB, virt), BF16),
             pltpu.VMEM((SLOTS, EB, EB, pairs), BF16),
-            pltpu.VMEM((pairs, virt), F32),
-            pltpu.VMEM((nv, rows, virt), F32),
+            pltpu.VMEM((2, side, side, rows, virt), F32),
+            pltpu.VMEM((side - 1, 2, side, rows, half), F32),
+            pltpu.VMEM((side - 1, 2, side, rows, half), F32),
+            pltpu.VMEM((2, side, rows, half), F32),
+            pltpu.VMEM((2, side, rows, half), F32),
+            pltpu.VMEM((2 * side - 1, rows, half), F32),
+            pltpu.VMEM((2 * side - 1, rows, half), F32),
             pltpu.VMEM((nocc, rows, virt), BF16),
             pltpu.VMEM((virt, cw), BF16),
             pltpu.VMEM((nv, rows, cw), BF16),
@@ -273,7 +323,7 @@
             pltpu.VMEM((EB * EB, EB * EB), BF16),
             dma((SLOTS,)), dma((8,)),
             dma((1,)), dma((nv,)), dma((1,)), dma((nv,)), dma((1,)), dma((nv,)),
-            dma((2,)), dma((2,)), dma((1,)), dma((1,)),
+            dma((2,)), dma((2,)), dma((4,)), dma((4,)),
         ],
         compiler_params=pltpu.CompilerParams(collective_id=0, has_side_effects=True, vmem_limit_bytes=56 * 2**20),
         cost_estimate=pl.CostEstimate(flops=flops, bytes_accessed=26_000_000, transcendentals=0),

time: 110 us -> 89.8 us (0.82)
  the two profiles are of different devices: /device:TPU:1 before, /device:TPU:8 now
where the time goes in v2:
time: 89.8 us; the launch traced here: 88.7 us
  Pallas kernels  87.2 us (97%)
  local copies, waits for them, and re-layouts  1.42 us (2%)
    pallas_call x1, Pallas kernels, on_device(): pl.pallas_call(functools.partial(kernel, side, side), out_shape=jax.Shape...  87.2 us

profile of v2, /device:TPU:8, one launch (start us, length us, event | category | flops | bytes accessed | tf_op | source)
XLA Modules:
  0.0 88.7 jit_solution(7915363199953769529)
XLA Ops:
  0.0 87.2 %ladder.1 = f32[24,512]{1,0:T(8,128)} custom-call(bf16[16,4096]{1,0:T(8,128)(2,1)} %r2.1, bf16[16,512,768]{2,1,0:T(8,128)(2,1)} %tau.1, bf16[16,512,512]{2,1,0:T(8,128)(2,1)} %w.1, bf16[24,4096]{1,0:T(8,128)(2,1)} %wo.1, bf16[64,24,512]{2,1,0:T(8,128)(2,1)} %wov.1, bf16[64,64]{1,0:T(8,128)(2,1)} %foo.1, bf16[512,512]{1,0:T(8,128)(2,1)} %fvv.1, ...), custom_call_target="tpu_custom_call" | custom-call | flops 9663676416 | bytes 26000000 | tf_op jit(solution)/shard_map/ladder/pallas_call | solution.py:300
  87.2 1.4 %copy.10 = f32[24,512]{1,0:T(8,128)} copy(f32[24,512]{1,0:T(8,128)} %ladder.1) | data formatting | bytes 98304

commit v3 on v2

--- a/solution.py
+++ b/solution.py
@@ -15,7 +15,8 @@
 LONG = 5
 SHARE = 3
 SLOTS = 8
-Z_LAG = 3
+AHEAD = 5
+Z_LAG = 5
 S_LAG = 3
 LAG = Z_LAG + S_LAG
 
@@ -36,7 +37,7 @@
     ny, nx,
     r2, tau, w, wo, wov, foo, fvv, r1,
     out,
-    wbuf, tbuf, acc, first_x, first_y, total_x, total_y, last_x, last_y, wovb, r2s, wos, foob, fvvb, winb, r1b, sing, perm,
+    wbuf, tbuf, acc, first_x, first_y, total_x, total_y, last_x, last_y, turned, cmat, wovb, r2s, wos, foob, fvvb, winb, r1b, sing, perm,
     tau_sem, loc_sem, long_send, long_recv, z_send, z_recv, sib_send, sib_recv, small_send, small_recv, rs_send, rs_recv,
 ):
     nv = 2 * ny * nx
@@ -92,6 +93,8 @@
     lax.fori_loop(1, nv, greet, 0)
     for other in (sibling, partner):
         pl.semaphore_signal(barrier, inc=1, device_id=other, device_id_type=MESH)
+    for j in range(SLOTS):
+        tau_copy(j).start()
     for copy in local:
         copy.start()
     pl.semaphore_wait(barrier, nv - 1 + nv // 2 + 2)
@@ -120,11 +123,16 @@
             device_id=(zd * 2 + c, v),
             device_id_type=MESH,
         ).start()
+        return 0
+
+    def send_small(j, _):
+        v, _zd = peer(j, 1)
         for copy in small_copies(v):
             copy.start()
         return 0
 
     lax.fori_loop(1, nv, send, 0)
+    lax.fori_loop(1, nv, send_small, 0)
 
     i, j = iotas(EB * EB, EB * EB)
     perm[...] = onehot(((i >> 4) == (j & 15)) & ((i & 15) == (j >> 4)))
@@ -150,23 +158,24 @@
     def received(ref, sem):
         pltpu.make_async_copy(ref, ref, sem).wait()
 
-    def compute(j):
+    def prepare(j):
         tau_copy(j).wait()
         block = tbuf[j % SLOTS].reshape(EB * EB, pairs)
-        turned = dot(perm[...], block, 1, 0).astype(BF16)
+        turned[j] = dot(block, perm[...], 0, 0).astype(BF16)
+
+        @pl.when(j + SLOTS < nv)
+        def _():
+            tau_copy(j + SLOTS).start()
+
+    def compute(j):
         weights = wbuf[j].reshape(EB * EB, virt)
         step = pairs // 2
         for part in range(2):
-            at = slice(part * step, (part + 1) * step)
-            acc[part] += dot(turned[:, at], weights, 0, 0).reshape(acc.shape[1:])
+            acc[part] += dot(turned[j, pl.ds(part * step, step)], weights, 1, 0).reshape(acc.shape[1:])
 
     def advance(j, _):
         k, t = j - Z_LAG, j - LAG
 
-        @pl.when(j < nv)
-        def _():
-            tau_copy(j).start()
-
         @pl.when((j >= 1) & (j < nv))
         def _():
             received(wbuf.at[j, pl.ds(HALF * c + SHARE * zl, LONG)], long_recv.at[j])
@@ -185,8 +194,17 @@
         def _():
             compute(lax.max(t, 0))
 
-        return 0
-
+        @pl.when(j + AHEAD < nv)
+        def _():
+            prepare(j + AHEAD)
+
+        return 0
+
+    def prepare_early(j, _):
+        prepare(j)
+        return 0
+
+    lax.fori_loop(0, AHEAD, prepare_early, 0)
     local[0].wait()
     middle = nv // 2
     lax.fori_loop(0, middle, advance, 0)
@@ -202,12 +220,6 @@
         sing[...] += factor * wovb[k].astype(F32)
 
     local[2].wait()
-    local[5].wait()
-    local[6].wait()
-    others = (nv - 1) * EB
-    received(r2s.at[pl.ds(0, others), :], small_recv.at[0])
-    received(wos.at[pl.ds(0, nv - 1)], small_recv.at[1])
-    held = r2s[...]
     fock = foob[...]
     m_first = me * (cw // nocc)
     i, j = iotas(nocc, cw)
@@ -217,13 +229,22 @@
     take_i = dot(onehot((p >> ob) == q), by_i, 1, 0)
     take_j = dot(onehot((p & (nocc - 1)) == q), by_j, 1, 0)
     p, q = iotas(pairs, cw)
-    first = jnp.where((p & (nocc - 1)) == (q & (nocc - 1)), take_i, 0.0).astype(BF16)
-    second = jnp.where((p >> ob) == (q >> ob) + m_first, take_j, 0.0).astype(BF16)
+    cmat[0] = jnp.where((p & (nocc - 1)) == (q & (nocc - 1)), take_i, 0.0).astype(BF16)
+    cmat[1] = jnp.where((p >> ob) == (q >> ob) + m_first, take_j, 0.0).astype(BF16)
+
+    lax.fori_loop(middle, nv, advance, 0)
+
+    local[5].wait()
+    local[6].wait()
+    others = (nv - 1) * EB
+    received(r2s.at[pl.ds(0, others), :], small_recv.at[0])
+    received(wos.at[pl.ds(0, nv - 1)], small_recv.at[1])
+    held = r2s[...]
     quartic = wos[...].astype(F32).reshape(pairs, cw).astype(BF16)
-    other_terms = dot(quartic, held, 1, 1) - dot(first, held, 1, 1) - dot(second, held, 1, 1)
+    other_terms = dot(quartic, held, 1, 1) - dot(cmat[0], held, 1, 1) - dot(cmat[1], held, 1, 1)
     acc[...] += other_terms.reshape(acc.shape)
 
-    lax.fori_loop(middle, nv + LAG, advance, 0)
+    lax.fori_loop(nv, nv + LAG, advance, 0)
 
     half = virt // 2
     left, right = pl.ds(0, half), pl.ds(half, half)
@@ -312,6 +333,8 @@
             pltpu.VMEM((2, side, rows, half), F32),
             pltpu.VMEM((2 * side - 1, rows, half), F32),
             pltpu.VMEM((2 * side - 1, rows, half), F32),
+            pltpu.VMEM((nv, pairs, EB * EB), BF16),
+            pltpu.VMEM((2, pairs, cw), BF16),
             pltpu.VMEM((nocc, rows, virt), BF16),
             pltpu.VMEM((virt, cw), BF16),
             pltpu.VMEM((nv, rows, cw), BF16),

time: 89.8 us -> 87.5 us (0.974)
  the two profiles are of different devices: /device:TPU:8 before, /device:TPU:24 now
where the time goes in v3:
time: 87.5 us; the launch traced here: 87.3 us
  Pallas kernels  85.9 us (98%)
  local copies, waits for them, and re-layouts  1.42 us (2%)
    pallas_call x1, Pallas kernels, on_device(): pl.pallas_call(functools.partial(kernel, side, side), out_shape=jax.Shape...  85.9 us

profile of v3, /device:TPU:24, one launch (start us, length us, event | category | flops | bytes accessed | tf_op | source)
XLA Modules:
  0.0 87.3 jit_solution(14088541679792398355)
XLA Ops:
  0.0 85.9 %ladder.1 = f32[24,512]{1,0:T(8,128)} custom-call(bf16[16,4096]{1,0:T(8,128)(2,1)} %r2.1, bf16[16,512,768]{2,1,0:T(8,128)(2,1)} %tau.1, bf16[16,512,512]{2,1,0:T(8,128)(2,1)} %w.1, bf16[24,4096]{1,0:T(8,128)(2,1)} %wo.1, bf16[64,24,512]{2,1,0:T(8,128)(2,1)} %wov.1, bf16[64,64]{1,0:T(8,128)(2,1)} %foo.1, bf16[512,512]{1,0:T(8,128)(2,1)} %fvv.1, ...), custom_call_target="tpu_custom_call" | custom-call | flops 9663676416 | bytes 26000000 | tf_op jit(solution)/shard_map/ladder/pallas_call | solution.py:321
  85.9 1.4 %copy.10 = f32[24,512]{1,0:T(8,128)} copy(f32[24,512]{1,0:T(8,128)} %ladder.1) | data formatting | bytes 98304

commit v4 on v3

--- a/solution.py
+++ b/solution.py
@@ -15,6 +15,7 @@
 LONG = 5
 SHARE = 3
 SLOTS = 8
+CHUNKS = 4
 AHEAD = 5
 Z_LAG = 5
 S_LAG = 3
@@ -37,7 +38,7 @@
     ny, nx,
     r2, tau, w, wo, wov, foo, fvv, r1,
     out,
-    wbuf, tbuf, acc, first_x, first_y, total_x, total_y, last_x, last_y, turned, cmat, wovb, r2s, wos, foob, fvvb, winb, r1b, sing, perm,
+    wbuf, tbuf, acc, near, total, far, turned, cmat, wovb, r2s, wos, foob, fvvb, winb, r1b, sing, perm,
     tau_sem, loc_sem, long_send, long_recv, z_send, z_recv, sib_send, sib_recv, small_send, small_recv, rs_send, rs_recv,
 ):
     nv = 2 * ny * nx
@@ -54,7 +55,7 @@
     partner = ((1 - zl) * 2 + c, me)
 
     def peer(j, sign):
-        k = (j * 13) % nv
+        k = (j * 11) % nv
         oz, oy, ox = k // (ny * nx), (k // nx) % ny, k % nx
         v = ((zh + oz) % 2) * (ny * nx) + ((y + sign * oy + ny) % ny) * nx + (x + sign * ox + nx) % nx
         return v, (zl + oz) % 2
@@ -141,7 +142,14 @@
     local[4].wait()
     i, j = iotas(EB, virt)
     chosen = dot(onehot(j == i + me * EB), fvvb[...], 1, 1).astype(BF16)
-    acc[...] = dot(winb[...], chosen, 0, 0).reshape(acc.shape)
+    columns = virt // CHUNKS
+
+    def add_terms(value, old):
+        for q in range(CHUNKS):
+            piece = value[:, q * columns : (q + 1) * columns].reshape(acc.shape[1:])
+            acc[q] = acc[q] + piece if old else piece
+
+    add_terms(dot(winb[...], chosen, 0, 0), False)
 
     def z_copy(j):
         part = wbuf.at[j, pl.ds(HALF * c + LONG * zl, SHARE)]
@@ -171,7 +179,9 @@
         weights = wbuf[j].reshape(EB * EB, virt)
         step = pairs // 2
         for part in range(2):
-            acc[part] += dot(turned[j, pl.ds(part * step, step)], weights, 1, 0).reshape(acc.shape[1:])
+            product = dot(turned[j, pl.ds(part * step, step)], weights, 1, 0)
+            for q in range(CHUNKS):
+                acc[q, part] += product[:, q * columns : (q + 1) * columns].reshape(acc.shape[2:])
 
     def advance(j, _):
         k, t = j - Z_LAG, j - LAG
@@ -241,81 +251,66 @@
     received(wos.at[pl.ds(0, nv - 1)], small_recv.at[1])
     held = r2s[...]
     quartic = wos[...].astype(F32).reshape(pairs, cw).astype(BF16)
-    other_terms = dot(quartic, held, 1, 1) - dot(cmat[0], held, 1, 1) - dot(cmat[1], held, 1, 1)
-    acc[...] += other_terms.reshape(acc.shape)
+    add_terms(dot(quartic, held, 1, 1) - dot(cmat[0], held, 1, 1) - dot(cmat[1], held, 1, 1), True)
 
     lax.fori_loop(nv, nv + LAG, advance, 0)
 
-    half = virt // 2
-    left, right = pl.ds(0, half), pl.ds(half, half)
+    side = nx
 
     def flat(z_at, y_at, x_at):
         return z_at * (ny * nx) + y_at * nx + x_at
 
-    def along_x(ox):
-        at = (x + ox) % nx
-        return pltpu.make_async_remote_copy(
-            src_ref=acc.at[:, :, at, :, left], dst_ref=first_x.at[ox - 1], send_sem=rs_send.at[0], recv_sem=rs_recv.at[0],
-            device_id=(root, flat(zh, y, at)), device_id_type=MESH,
-        )
-
-    def along_y(oy):
-        at = (y + oy) % ny
-        return pltpu.make_async_remote_copy(
-            src_ref=acc.at[:, at, :, :, right], dst_ref=first_y.at[oy - 1], send_sem=rs_send.at[1], recv_sem=rs_recv.at[1],
-            device_id=(root, flat(zh, at, x)), device_id_type=MESH,
-        )
-
-    for offset in range(1, max(nx, ny)):
-        if offset < nx:
-            along_x(offset).start()
-        if offset < ny:
-            along_y(offset).start()
-
-    received(first_x, rs_recv.at[0])
-    total_x[...] = acc[:, :, x, :, :half] + jnp.sum(first_x[...], axis=0)
-
-    def to_owner_x(q, _):
-        z_at, y_at = (zh + q // ny) % 2, (y + q % ny) % ny
-        pltpu.make_async_remote_copy(
-            src_ref=total_x.at[z_at, y_at], dst_ref=last_x.at[q - 1], send_sem=rs_send.at[2], recv_sem=rs_recv.at[2],
-            device_id=(root, flat(z_at, y_at, x)), device_id_type=MESH,
-        ).start()
-        return 0
-
-    lax.fori_loop(1, 2 * ny, to_owner_x, 0)
-    received(first_y, rs_recv.at[1])
-    total_y[...] = acc[:, y, :, :, half:] + jnp.sum(first_y[...], axis=0)
-
-    def to_owner_y(q, _):
-        z_at, x_at = (zh + q // nx) % 2, (x + q % nx) % nx
-        pltpu.make_async_remote_copy(
-            src_ref=total_y.at[z_at, x_at], dst_ref=last_y.at[q - 1], send_sem=rs_send.at[3], recv_sem=rs_recv.at[3],
-            device_id=(root, flat(z_at, y, x_at)), device_id_type=MESH,
-        ).start()
-        return 0
-
-    lax.fori_loop(1, 2 * nx, to_owner_y, 0)
+    def line(q, at):
+        return acc.at[q, :, at] if q % 2 else acc.at[q, :, :, at]
+
+    def here(q):
+        return y if q % 2 else x
+
+    def cross(q):
+        return x if q % 2 else y
+
+    for q in range(CHUNKS):
+        for offset in range(1, side):
+            at = (here(q) + offset) % side
+            pltpu.make_async_remote_copy(
+                src_ref=line(q, at), dst_ref=near.at[q, offset - 1], send_sem=rs_send.at[q], recv_sem=rs_recv.at[q],
+                device_id=(root, flat(zh, at, x) if q % 2 else flat(zh, y, at)), device_id_type=MESH,
+            ).start()
+
+    for q in range(CHUNKS):
+        received(near.at[q], rs_recv.at[q])
+        total[q] = line(q, here(q))[...] + jnp.sum(near[q], axis=0)
+
+        def to_owner(i, _, q=q):
+            z_at, at = (zh + i // side) % 2, (cross(q) + i % side) % side
+            pltpu.make_async_remote_copy(
+                src_ref=total.at[q, z_at, at], dst_ref=far.at[q, i - 1],
+                send_sem=rs_send.at[CHUNKS + q], recv_sem=rs_recv.at[CHUNKS + q],
+                device_id=(root, flat(z_at, y, at) if q % 2 else flat(z_at, at, x)), device_id_type=MESH,
+            ).start()
+            return 0
+
+        lax.fori_loop(1, 2 * side, to_owner, 0)
+
     received(wbuf.at[pl.ds(0, nv - 1), pl.ds(0, LONG)], long_send.at[0])
     received(wbuf.at[pl.ds(0, nv - 1), pl.ds(0, SHARE)], z_send.at[0])
     received(wbuf.at[pl.ds(0, nv - 1), pl.ds(0, HALF)], sib_send.at[0])
     received(r2s.at[pl.ds(0, others), :], small_send.at[0])
     received(wos.at[pl.ds(0, nv - 1)], small_send.at[1])
-    received(first_x, rs_send.at[0])
-    received(first_y, rs_send.at[1])
-    received(last_x, rs_recv.at[2])
-    out[:, :half] = total_x[zh, y] - sing[:, :half] + jnp.sum(last_x[...], axis=0)
-    received(last_y, rs_recv.at[3])
-    out[:, half:] = total_y[zh, x] - sing[:, half:] + jnp.sum(last_y[...], axis=0)
-    received(last_x, rs_send.at[2])
-    received(last_y, rs_send.at[3])
+    for q in range(CHUNKS):
+        cols = slice(q * columns, (q + 1) * columns)
+        received(far.at[q], rs_recv.at[CHUNKS + q])
+        out[:, cols] = total[q, zh, cross(q)] - sing[:, cols] + jnp.sum(far[q], axis=0)
+    for q in range(CHUNKS):
+        received(near.at[q], rs_send.at[q])
+        received(far.at[q], rs_send.at[CHUNKS + q])
 
 
 def on_device(r2, tau, w, wo, wov, foo, fvv, r1):
     nv = w.shape[1] // w.shape[0]
     side = int(math.isqrt(nv // 2))
     rows, virt, pairs, nocc = wo.shape[0], w.shape[2], tau.shape[2], foo.shape[0]
-    cw, half = wo.shape[1] // nv, virt // 2
+    cw, columns = wo.shape[1] // nv, virt // CHUNKS
     dma = pltpu.SemaphoreType.DMA
     flops = 2 * nv * EB * EB * pairs * (virt + EB * EB)
     return pl.pallas_call(
@@ -326,13 +321,10 @@
         scratch_shapes=[
             pltpu.VMEM((nv, EB, EB, virt), BF16),
             pltpu.VMEM((SLOTS, EB, EB, pairs), BF16),
-            pltpu.VMEM((2, side, side, rows, virt), F32),
-            pltpu.VMEM((side - 1, 2, side, rows, half), F32),
-            pltpu.VMEM((side - 1, 2, side, rows, half), F32),
-            pltpu.VMEM((2, side, rows, half), F32),
-            pltpu.VMEM((2, side, rows, half), F32),
-            pltpu.VMEM((2 * side - 1, rows, half), F32),
-            pltpu.VMEM((2 * side - 1, rows, half), F32),
+            pltpu.VMEM((CHUNKS, 2, side, side, rows, columns), F32),
+            pltpu.VMEM((CHUNKS, side - 1, 2, side, rows, columns), F32),
+            pltpu.VMEM((CHUNKS, 2, side, rows, columns), F32),
+            pltpu.VMEM((CHUNKS, 2 * side - 1, rows, columns), F32),
             pltpu.VMEM((nv, pairs, EB * EB), BF16),
             pltpu.VMEM((2, pairs, cw), BF16),
             pltpu.VMEM((nocc, rows, virt), BF16),
@@ -346,7 +338,7 @@
             pltpu.VMEM((EB * EB, EB * EB), BF16),
             dma((SLOTS,)), dma((8,)),
             dma((1,)), dma((nv,)), dma((1,)), dma((nv,)), dma((1,)), dma((nv,)),
-            dma((2,)), dma((2,)), dma((4,)), dma((4,)),
+            dma((2,)), dma((2,)), dma((2 * CHUNKS,)), dma((2 * CHUNKS,)),
         ],
         compiler_params=pltpu.CompilerParams(collective_id=0, has_side_effects=True, vmem_limit_bytes=56 * 2**20),
         cost_estimate=pl.CostEstimate(flops=flops, bytes_accessed=26_000_000, transcendentals=0),

time: 87.5 us -> 81.9 us (0.936)
  the two profiles are of different devices: /device:TPU:24 before, /device:TPU:8 now
where the time goes in v4:
time: 81.9 us; the launch traced here: 81.7 us
  Pallas kernels  80.3 us (98%)
  local copies, waits for them, and re-layouts  1.42 us (2%)
    pallas_call x1, Pallas kernels, on_device(): pl.pallas_call(functools.partial(kernel, side, side), out_shape=jax.Shape...  80.3 us

profile of v4, /device:TPU:8, one launch (start us, length us, event | category | flops | bytes accessed | tf_op | source)
XLA Modules:
  0.0 81.7 jit_solution(3849667038420301756)
XLA Ops:
  0.0 80.3 %ladder.1 = f32[24,512]{1,0:T(8,128)} custom-call(bf16[16,4096]{1,0:T(8,128)(2,1)} %r2.1, bf16[16,512,768]{2,1,0:T(8,128)(2,1)} %tau.1, bf16[16,512,512]{2,1,0:T(8,128)(2,1)} %w.1, bf16[24,4096]{1,0:T(8,128)(2,1)} %wo.1, bf16[64,24,512]{2,1,0:T(8,128)(2,1)} %wov.1, bf16[64,64]{1,0:T(8,128)(2,1)} %foo.1, bf16[512,512]{1,0:T(8,128)(2,1)} %fvv.1, ...), custom_call_target="tpu_custom_call" | custom-call | flops 9663676416 | bytes 26000000 | tf_op jit(solution)/shard_map/ladder/pallas_call | solution.py:316
  80.3 1.4 %copy.10 = f32[24,512]{1,0:T(8,128)} copy(f32[24,512]{1,0:T(8,128)} %ladder.1) | data formatting | bytes 98304

commit v5 on v4

--- a/solution.py
+++ b/solution.py
@@ -15,6 +15,7 @@
 LONG = 5
 SHARE = 3
 SLOTS = 8
+UNDER = 12
 CHUNKS = 4
 AHEAD = 5
 Z_LAG = 5
@@ -42,11 +43,14 @@
     tau_sem, loc_sem, long_send, long_recv, z_send, z_recv, sib_send, sib_recv, small_send, small_recv, rs_send, rs_recv,
 ):
     nv = 2 * ny * nx
+    rounds = nv - 1
+    steps = 2 * rounds
     nocc = foo.shape[0]
     pairs = tau.shape[2]
     rows = pairs // nv
     cw = wo.shape[1] // nv
     virt = fvv.shape[0]
+    half = virt // 2
     ob = int(math.log2(nocc))
     root, me = lax.axis_index("root"), lax.axis_index("virt")
     zl, c = root // 2, root % 2
@@ -69,7 +73,7 @@
     mine = pl.ds(pl.multiple_of(me * EB, EB), EB)
     my_cols = pl.ds(pl.multiple_of(me * cw, cw), cw)
     local = [
-        pltpu.make_async_copy(w.at[:, mine, :], wbuf.at[0], loc_sem.at[0]),
+        pltpu.make_async_copy(w.at[:, mine, pl.ds(0, half)], wbuf.at[steps], loc_sem.at[0]),
         pltpu.make_async_copy(wov, wovb, loc_sem.at[1]),
         pltpu.make_async_copy(foo, foob, loc_sem.at[2]),
         pltpu.make_async_copy(fvv, fvvb, loc_sem.at[3]),
@@ -77,6 +81,7 @@
         pltpu.make_async_copy(r2.at[:, my_cols], r2s.at[mine, :], loc_sem.at[5]),
         pltpu.make_async_copy(wo.at[:, my_cols], wos.at[me], loc_sem.at[6]),
         pltpu.make_async_copy(r1, r1b, loc_sem.at[7]),
+        pltpu.make_async_copy(w.at[:, mine, pl.ds(half, half)], wbuf.at[steps + 1], loc_sem.at[8]),
     ]
 
     barrier = pltpu.get_barrier_semaphore()
@@ -113,14 +118,15 @@
             ),
         )
 
-    def send(j, _):
-        v, zd = peer(j, 1)
+    def send(step, _):
+        v, zd = peer(step % rounds + 1, 1)
         first = HALF * c + SHARE * zd
+        cols = pl.ds(pl.multiple_of((step // rounds) * half, half), half)
         pltpu.make_async_remote_copy(
-            src_ref=w.at[pl.ds(first, LONG), pl.ds(pl.multiple_of(v * EB, EB), EB), :],
-            dst_ref=wbuf.at[j, pl.ds(first, LONG)],
+            src_ref=w.at[pl.ds(first, LONG), pl.ds(pl.multiple_of(v * EB, EB), EB), cols],
+            dst_ref=wbuf.at[step, pl.ds(first, LONG)],
             send_sem=long_send.at[0],
-            recv_sem=long_recv.at[j],
+            recv_sem=long_recv.at[step],
             device_id=(zd * 2 + c, v),
             device_id_type=MESH,
         ).start()
@@ -132,8 +138,9 @@
             copy.start()
         return 0
 
-    lax.fori_loop(1, nv, send, 0)
+    lax.fori_loop(0, rounds, send, 0)
     lax.fori_loop(1, nv, send_small, 0)
+    lax.fori_loop(rounds, steps, send, 0)
 
     i, j = iotas(EB * EB, EB * EB)
     perm[...] = onehot(((i >> 4) == (j & 15)) & ((i & 15) == (j >> 4)))
@@ -175,38 +182,36 @@
         def _():
             tau_copy(j + SLOTS).start()
 
-    def compute(j):
-        weights = wbuf[j].reshape(EB * EB, virt)
-        step = pairs // 2
+    def compute(j, slot, h):
+        weights = wbuf[slot].reshape(EB * EB, half)
+        size = pairs // 2
         for part in range(2):
-            product = dot(turned[j, pl.ds(part * step, step)], weights, 1, 0)
-            for q in range(CHUNKS):
-                acc[q, part] += product[:, q * columns : (q + 1) * columns].reshape(acc.shape[2:])
-
-    def advance(j, _):
-        k, t = j - Z_LAG, j - LAG
-
-        @pl.when((j >= 1) & (j < nv))
-        def _():
-            received(wbuf.at[j, pl.ds(HALF * c + SHARE * zl, LONG)], long_recv.at[j])
-            z_copy(j).start()
-
-        @pl.when((k >= 1) & (k < nv))
+            product = dot(turned[j, pl.ds(part * size, size)], weights, 1, 0)
+            for q in range(CHUNKS // 2):
+                acc[h * (CHUNKS // 2) + q, part] += product[:, q * columns : (q + 1) * columns].reshape(acc.shape[2:])
+
+    def advance(i, _):
+        k, t = i - Z_LAG, i - LAG
+
+        @pl.when(i < steps)
+        def _():
+            received(wbuf.at[i, pl.ds(HALF * c + SHARE * zl, LONG)], long_recv.at[i])
+            z_copy(i).start()
+
+        @pl.when((k >= 0) & (k < steps))
         def _():
             received(wbuf.at[k, pl.ds(HALF * c + LONG * (1 - zl), SHARE)], z_recv.at[k])
             sib_copy(k).start()
 
-        @pl.when(t > 0)
-        def _():
-            received(wbuf.at[t, pl.ds(HALF * (1 - c), HALF)], sib_recv.at[t])
-
         @pl.when(t >= 0)
         def _():
-            compute(lax.max(t, 0))
-
-        @pl.when(j + AHEAD < nv)
-        def _():
-            prepare(j + AHEAD)
+            at = lax.max(t, 0)
+            received(wbuf.at[at, pl.ds(HALF * (1 - c), HALF)], sib_recv.at[at])
+            compute(at % rounds + 1, at, at // rounds)
+
+        @pl.when(i + AHEAD < nv)
+        def _():
+            prepare(i + AHEAD)
 
         return 0
 
@@ -216,6 +221,9 @@
 
     lax.fori_loop(0, AHEAD, prepare_early, 0)
     local[0].wait()
+    local[8].wait()
+    for h in range(2):
+        compute(0, steps + h, h)
     middle = nv // 2
     lax.fori_loop(0, middle, advance, 0)
 
@@ -242,7 +250,7 @@
     cmat[0] = jnp.where((p & (nocc - 1)) == (q & (nocc - 1)), take_i, 0.0).astype(BF16)
     cmat[1] = jnp.where((p >> ob) == (q >> ob) + m_first, take_j, 0.0).astype(BF16)
 
-    lax.fori_loop(middle, nv, advance, 0)
+    lax.fori_loop(middle, rounds + LAG, advance, 0)
 
     local[5].wait()
     local[6].wait()
@@ -253,8 +261,6 @@
     quartic = wos[...].astype(F32).reshape(pairs, cw).astype(BF16)
     add_terms(dot(quartic, held, 1, 1) - dot(cmat[0], held, 1, 1) - dot(cmat[1], held, 1, 1), True)
 
-    lax.fori_loop(nv, nv + LAG, advance, 0)
-
     side = nx
 
     def flat(z_at, y_at, x_at):
@@ -269,7 +275,7 @@
     def cross(q):
         return x if q % 2 else y
 
-    for q in range(CHUNKS):
+    def to_line(q):
         for offset in range(1, side):
             at = (here(q) + offset) % side
             pltpu.make_async_remote_copy(
@@ -277,11 +283,11 @@
                 device_id=(root, flat(zh, at, x) if q % 2 else flat(zh, y, at)), device_id_type=MESH,
             ).start()
 
-    for q in range(CHUNKS):
+    def to_owners(q):
         received(near.at[q], rs_recv.at[q])
         total[q] = line(q, here(q))[...] + jnp.sum(near[q], axis=0)
 
-        def to_owner(i, _, q=q):
+        def to_owner(i, _):
             z_at, at = (zh + i // side) % 2, (cross(q) + i % side) % side
             pltpu.make_async_remote_copy(
                 src_ref=total.at[q, z_at, at], dst_ref=far.at[q, i - 1],
@@ -292,9 +298,21 @@
 
         lax.fori_loop(1, 2 * side, to_owner, 0)
 
-    received(wbuf.at[pl.ds(0, nv - 1), pl.ds(0, LONG)], long_send.at[0])
-    received(wbuf.at[pl.ds(0, nv - 1), pl.ds(0, SHARE)], z_send.at[0])
-    received(wbuf.at[pl.ds(0, nv - 1), pl.ds(0, HALF)], sib_send.at[0])
+    ready, over = rounds + LAG, steps + LAG
+    for q in range(CHUNKS // 2):
+        to_line(q)
+    lax.fori_loop(ready, min(ready + UNDER, over), advance, 0)
+    for q in range(CHUNKS // 2):
+        to_owners(q)
+    lax.fori_loop(min(ready + UNDER, over), over, advance, 0)
+    for q in range(CHUNKS // 2, CHUNKS):
+        to_line(q)
+    for q in range(CHUNKS // 2, CHUNKS):
+        to_owners(q)
+
+    received(wbuf.at[pl.ds(0, steps), pl.ds(0, LONG)], long_send.at[0])
+    received(wbuf.at[pl.ds(0, steps), pl.ds(0, SHARE)], z_send.at[0])
+    received(wbuf.at[pl.ds(0, steps), pl.ds(0, HALF)], sib_send.at[0])
     received(r2s.at[pl.ds(0, others), :], small_send.at[0])
     received(wos.at[pl.ds(0, nv - 1)], small_send.at[1])
     for q in range(CHUNKS):
@@ -319,7 +337,7 @@
         in_specs=[pl.BlockSpec(memory_space=pl.ANY)] * 8,
         out_specs=pl.BlockSpec(memory_space=pltpu.VMEM),
         scratch_shapes=[
-            pltpu.VMEM((nv, EB, EB, virt), BF16),
+            pltpu.VMEM((2 * nv, EB, EB, virt // 2), BF16),
             pltpu.VMEM((SLOTS, EB, EB, pairs), BF16),
             pltpu.VMEM((CHUNKS, 2, side, side, rows, columns), F32),
             pltpu.VMEM((CHUNKS, side - 1, 2, side, rows, columns), F32),
@@ -336,8 +354,8 @@
             pltpu.VMEM((1, nocc), BF16),
             pltpu.VMEM((rows, virt), F32),
             pltpu.VMEM((EB * EB, EB * EB), BF16),
-            dma((SLOTS,)), dma((8,)),
-            dma((1,)), dma((nv,)), dma((1,)), dma((nv,)), dma((1,)), dma((nv,)),
+            dma((SLOTS,)), dma((9,)),
+            dma((1,)), dma((2 * nv,)), dma((1,)), dma((2 * nv,)), dma((1,)), dma((2 * nv,)),
             dma((2,)), dma((2,)), dma((2 * CHUNKS,)), dma((2 * CHUNKS,)),
         ],
         compiler_params=pltpu.CompilerParams(collective_id=0, has_side_effects=True, vmem_limit_bytes=56 * 2**20),

time: 81.9 us -> 76.8 us (0.938)
  Pallas kernels: 80.3 us -> 74.8 us
    pallas_call x1, Pallas kernels: 80.3 us -> 74.8 us  [on_device(): pl.pallas_call(functools.partial(kernel, side, side), out_shape=jax.Shape...]
where the time goes in v5:
time: 76.8 us; the launch traced here: 76.2 us
  Pallas kernels  74.8 us (97%)
  local copies, waits for them, and re-layouts  1.42 us (2%)
    pallas_call x1, Pallas kernels, on_device(): pl.pallas_call(functools.partial(kernel, side, side), out_shape=jax.Shape...  74.8 us

profile of v5, /device:TPU:8, one launch (start us, length us, event | category | flops | bytes accessed | tf_op | source)
XLA Modules:
  0.0 76.2 jit_solution(1838557989413157453)
XLA Ops:
  0.0 74.8 %ladder.1 = f32[24,512]{1,0:T(8,128)} custom-call(bf16[16,4096]{1,0:T(8,128)(2,1)} %r2.1, bf16[16,512,768]{2,1,0:T(8,128)(2,1)} %tau.1, bf16[16,512,512]{2,1,0:T(8,128)(2,1)} %w.1, bf16[24,4096]{1,0:T(8,128)(2,1)} %wo.1, bf16[64,24,512]{2,1,0:T(8,128)(2,1)} %wov.1, bf16[64,64]{1,0:T(8,128)(2,1)} %foo.1, bf16[512,512]{1,0:T(8,128)(2,1)} %fvv.1, ...), custom_call_target="tpu_custom_call" | custom-call | flops 9663676416 | bytes 26000000 | tf_op jit(solution)/shard_map/ladder/pallas_call | solution.py:334
  74.8 1.4 %copy.10 = f32[24,512]{1,0:T(8,128)} copy(f32[24,512]{1,0:T(8,128)} %ladder.1) | data formatting | bytes 98304

commit v6 on v5

--- a/solution.py
+++ b/solution.py
@@ -15,11 +15,11 @@
 LONG = 5
 SHARE = 3
 SLOTS = 8
-UNDER = 12
+UNDER = 18
 CHUNKS = 4
 AHEAD = 5
-Z_LAG = 5
-S_LAG = 3
+Z_LAG = 12
+S_LAG = 5
 LAG = Z_LAG + S_LAG
 
 

time: 76.8 us -> 74.4 us (0.969)
  Pallas kernels: 74.8 us -> 72.8 us
    pallas_call x1, Pallas kernels: 74.8 us -> 72.8 us  [on_device(): pl.pallas_call(functools.partial(kernel, side, side), out_shape=jax.Shape...]
where the time goes in v6:
time: 74.4 us; the launch traced here: 74.2 us
  Pallas kernels  72.8 us (98%)
  local copies, waits for them, and re-layouts  1.42 us (2%)
    pallas_call x1, Pallas kernels, on_device(): pl.pallas_call(functools.partial(kernel, side, side), out_shape=jax.Shape...  72.8 us

profile of v6, /device:TPU:8, one launch (start us, length us, event | category | flops | bytes accessed | tf_op | source)
XLA Modules:
  0.0 74.2 jit_solution(11602658333613125797)
XLA Ops:
  0.0 72.8 %ladder.1 = f32[24,512]{1,0:T(8,128)} custom-call(bf16[16,4096]{1,0:T(8,128)(2,1)} %r2.1, bf16[16,512,768]{2,1,0:T(8,128)(2,1)} %tau.1, bf16[16,512,512]{2,1,0:T(8,128)(2,1)} %w.1, bf16[24,4096]{1,0:T(8,128)(2,1)} %wo.1, bf16[64,24,512]{2,1,0:T(8,128)(2,1)} %wov.1, bf16[64,64]{1,0:T(8,128)(2,1)} %foo.1, bf16[512,512]{1,0:T(8,128)(2,1)} %fvv.1, ...), custom_call_target="tpu_custom_call" | custom-call | flops 9663676416 | bytes 26000000 | tf_op jit(solution)/shard_map/ladder/pallas_call | solution.py:334
  72.8 1.4 %copy.10 = f32[24,512]{1,0:T(8,128)} copy(f32[24,512]{1,0:T(8,128)} %ladder.1) | data formatting | bytes 98304

commit v7 on v6

--- a/solution.py
+++ b/solution.py
@@ -227,16 +227,6 @@
     middle = nv // 2
     lax.fori_loop(0, middle, advance, 0)
 
-    local[1].wait()
-    local[7].wait()
-    i, j = iotas(nocc, nocc)
-    spread = jnp.where(i == j, jnp.broadcast_to(r1b[...].astype(F32), (nocc, nocc)), 0.0).astype(BF16)
-    winb32 = dot(spread, jnp.ones((nocc, 128), BF16), 1, 0)
-    sing[...] = jnp.zeros_like(sing)
-    for k in range(nocc):
-        factor = jnp.broadcast_to(winb32[k : k + 1, 0:1], (rows, virt))
-        sing[...] += factor * wovb[k].astype(F32)
-
     local[2].wait()
     fock = foob[...]
     m_first = me * (cw // nocc)
@@ -307,6 +297,17 @@
     lax.fori_loop(min(ready + UNDER, over), over, advance, 0)
     for q in range(CHUNKS // 2, CHUNKS):
         to_line(q)
+
+    local[1].wait()
+    local[7].wait()
+    i, j = iotas(nocc, nocc)
+    spread = jnp.where(i == j, jnp.broadcast_to(r1b[...].astype(F32), (nocc, nocc)), 0.0).astype(BF16)
+    winb32 = dot(spread, jnp.ones((nocc, 128), BF16), 1, 0)
+    sing[...] = jnp.zeros_like(sing)
+    for k in range(nocc):
+        factor = jnp.broadcast_to(winb32[k : k + 1, 0:1], (rows, virt))
+        sing[...] += factor * wovb[k].astype(F32)
+
     for q in range(CHUNKS // 2, CHUNKS):
         to_owners(q)
 

time: 74.4 us -> 74.4 us (level)
  no operation moved by 1% of the time
where the time goes in v7:
time: 74.4 us; the launch traced here: 74.2 us
  Pallas kernels  72.8 us (98%)
  local copies, waits for them, and re-layouts  1.42 us (2%)
    pallas_call x1, Pallas kernels, on_device(): pl.pallas_call(functools.partial(kernel, side, side), out_shape=jax.Shape...  72.8 us

profile of v7, /device:TPU:8, one launch (start us, length us, event | category | flops | bytes accessed | tf_op | source)
XLA Modules:
  0.0 74.2 jit_solution(15701536680778063335)
XLA Ops:
  0.0 72.8 %ladder.1 = f32[24,512]{1,0:T(8,128)} custom-call(bf16[16,4096]{1,0:T(8,128)(2,1)} %r2.1, bf16[16,512,768]{2,1,0:T(8,128)(2,1)} %tau.1, bf16[16,512,512]{2,1,0:T(8,128)(2,1)} %w.1, bf16[24,4096]{1,0:T(8,128)(2,1)} %wo.1, bf16[64,24,512]{2,1,0:T(8,128)(2,1)} %wov.1, bf16[64,64]{1,0:T(8,128)(2,1)} %foo.1, bf16[512,512]{1,0:T(8,128)(2,1)} %fvv.1, ...), custom_call_target="tpu_custom_call" | custom-call | flops 9663676416 | bytes 26000000 | tf_op jit(solution)/shard_map/ladder/pallas_call | solution.py:335
  72.8 1.4 %copy.10 = f32[24,512]{1,0:T(8,128)} copy(f32[24,512]{1,0:T(8,128)} %ladder.1) | data formatting | bytes 98304
